TPU v7x, 256 devices: a whole 4x4x8 slice. The times are simulated.
256 devices in a mesh: fsdp: 16 (over y, x), tensor: 16 (over z, core).
Axes of the slice: x: 4, y: 4, z: 8, core: 2. Of those that a mesh axis runs over, the one named last changes fastest.
Arguments:
- inputs: bfloat16 [3072, 8192], P('fsdp'), may hold values from -6 to 6
- cotangent: bfloat16 [3072, 8192], P('fsdp'), may hold values from -1.1953125 to 1.1953125
- up_tiles: bfloat16 [16, 64, 128, 128], P('tensor', 'fsdp'), may hold values from -0.25 to 0.25
- up_rows: int32 [16, 64], P('tensor', 'fsdp'), may hold values from 0 to 63, as said below
- up_cols: int32 [16, 64], P('tensor', 'fsdp'), may hold values from 0 to 15, as said below
- down_tiles: bfloat16 [16, 64, 128, 128], P('tensor', 'fsdp'), may hold values from -0.25 to 0.25
- down_rows: int32 [16, 64], P('tensor', 'fsdp'), may hold values from 0 to 15, as said below
- down_cols: int32 [16, 64], P('tensor', 'fsdp'), may hold values from 0 to 63, as said below
Outputs:
- input_grad: bfloat16 [3072, 8192], P('fsdp', 'tensor')
- up_grad: bfloat16 [16, 64, 128, 128], P('tensor', 'fsdp')
- down_grad: bfloat16 [16, 64, 128, 128], P('tensor', 'fsdp')
Inputs may be any that keep to these rules, and one draw needn't show every extreme that they name: `up_rows`: together with up_cols, the positions of a group's 64 tiles are distinct; slot s is held by fsdp index s // 4. `up_cols`: see up_rows. `down_rows`: together with down_cols, the positions of a group's 64 tiles are distinct; slot s is held by fsdp index s // 4. `down_cols`: see down_rows.
All inputs are finite; a program needn't handle non-finite values.
Results may differ from a plain program's by a relative error of at most 0.015.
Values may be sent and summed in bfloat16 or wider, within the bound.
A program may use at most 128 MiB of HBM per device.

v0:
```python
import jax
import jax.numpy as jnp
from jax import lax
from jax.sharding import PartitionSpec as P

FF = 32768
TILE = 128


def gelu_parts(pre):
    coef = 0.7978845608028654
    inner = coef * (pre + 0.044715 * pre * pre * pre)
    tanh_val = jnp.tanh(inner)
    act = 0.5 * pre * (1.0 + tanh_val)
    slope = 0.5 * (1.0 + tanh_val) + 0.5 * pre * (1.0 - tanh_val * tanh_val) * coef * (
        1.0 + 3.0 * 0.044715 * pre * pre
    )
    return (act, slope)


def on_device(inputs, cotangent, up_tiles, up_rows, up_cols, down_tiles, down_rows, down_cols):
    tok_count = inputs.shape[0]
    row_blocks = inputs.shape[1] // TILE
    group_cols = FF // (lax.axis_size("tensor") * TILE)
    input_blocks = inputs.reshape(tok_count, row_blocks, TILE)
    cotan_blocks = cotangent.reshape(tok_count, row_blocks, TILE)
    gathered = (
        lax.all_gather(up_tiles, "fsdp", axis=1, tiled=True),
        lax.all_gather(up_rows, "fsdp", axis=1, tiled=True),
        lax.all_gather(up_cols, "fsdp", axis=1, tiled=True),
        lax.all_gather(down_tiles, "fsdp", axis=1, tiled=True),
        lax.all_gather(down_rows, "fsdp", axis=1, tiled=True),
        lax.all_gather(down_cols, "fsdp", axis=1, tiled=True),
    )
    w_up, r_up, c_up = (gathered[0][0], gathered[1][0], gathered[2][0])
    w_down, r_down, c_down = (gathered[3][0], gathered[4][0], gathered[5][0])
    x_sel = jnp.take(input_blocks, r_up, axis=1)
    prod = jnp.einsum("tsk,skf->stf", x_sel, w_up, preferred_element_type=jnp.float32)
    pre = jax.ops.segment_sum(prod, c_up, num_segments=group_cols)
    act, slope = gelu_parts(pre)
    hidden = act.astype(jnp.bfloat16)
    dy_sel = jnp.take(cotan_blocks, c_down, axis=1)
    h_sel = jnp.take(hidden, r_down, axis=0)
    back = jnp.einsum("tsk,sfk->stf", dy_sel, w_down, preferred_element_type=jnp.float32)
    dhid = jax.ops.segment_sum(back, r_down, num_segments=group_cols)
    dpre = (dhid * slope).astype(jnp.bfloat16)
    dp_sel = jnp.take(dpre, c_up, axis=0)
    both_sum = lax.psum_scatter(
        jnp.stack(
            [
                jnp.einsum("tsk,stf->skf", x_sel, dp_sel, preferred_element_type=jnp.float32),
                jnp.einsum("stf,tsk->sfk", h_sel, dy_sel, preferred_element_type=jnp.float32),
            ],
            axis=1,
        ).astype(jnp.bfloat16),
        "fsdp",
        scatter_dimension=0,
        tiled=True,
    ).astype(jnp.float32)
    up_sum = both_sum[:, 0]
    down_sum = both_sum[:, 1]
    back_in = jnp.einsum("stf,skf->stk", dp_sel, w_up, preferred_element_type=jnp.float32)
    in_part = jax.ops.segment_sum(back_in, r_up, num_segments=row_blocks)
    own_blocks = lax.psum_scatter(
        in_part.astype(jnp.bfloat16), "tensor", scatter_dimension=0, tiled=True
    ).astype(jnp.float32)
    input_grad = jnp.transpose(own_blocks, (1, 0, 2)).reshape(tok_count, -1).astype(jnp.bfloat16)
    up_grad = up_sum.astype(jnp.bfloat16)[None]
    down_grad = down_sum.astype(jnp.bfloat16)[None]
    return (input_grad, up_grad, down_grad)


def solution(mesh):
    placed = (
        P("fsdp", None),
        P("fsdp", None),
        P("tensor", "fsdp", None, None),
        P("tensor", "fsdp"),
        P("tensor", "fsdp"),
        P("tensor", "fsdp", None, None),
        P("tensor", "fsdp"),
        P("tensor", "fsdp"),
    )
    return jax.shard_map(
        on_device,
        mesh=mesh,
        in_specs=placed,
        out_specs=(
            P("fsdp", "tensor"),
            P("tensor", "fsdp", None, None),
            P("tensor", "fsdp", None, None),
        ),
        check_vma=False,
    )
```

profile of v0, /device:TPU:2, one launch (start us, length us, event | category | flops | bytes accessed | tf_op | source)
XLA Modules:
  0.0 336.9 jit_solution(617230634421711850)
XLA Ops:
  13.7 15.6 %all-reduce.5 = (s32[64]{0:T(128)S(1)}, s32[64]{0:T(128)S(1)}, s32[64]{0:T(128)S(1)}, s32[64]{0:T(128)S(1)}) all-reduce(s32[64]{0:T(128)S(1)} %bitcast_dynamic-update-slice_fusion.3, s32[64]{0:T(128)S(1)} %bitcast_dynamic-update-slice_fusion.1, s32[64]{0:T(128)S(1)} %bitcast_dynamic-update-slice_fusion, ...), channel_id=1, replica_groups=mesh['fsdp'=16,'tensor'=16] {'fsdp'}, use_global_device_ids=true, to_apply=%add | all-reduce | flops 256 | bytes 2048 | tf_op jit(solution)/shard_map/broadcast_in_dim;squeeze | solution.py:63
  29.4 2.5 copy_bitcast_fusion
  31.9 4.5 %gather_fusion.1 = bf16[64,192,128]{2,1,0:T(8,128)(2,1)} fusion(bf16[192,64,128]{2,0,1:T(8,128)(2,1)} %copy_bitcast_fusion, s32[1024]{0:T(1024)S(1)} %pad_clamp_fusion.2), kind=kCustom, calls=%fused_computation.2.clone | custom fusion | bytes 6291712 | tf_op jit(solution)/shard_map/jit(_take)/gather | solution.py:37
  36.4 2.8 copy_bitcast_fusion.1
  39.2 2.6 gather_fusion
  41.9 21.2 %all-gather.5.cloned.1.call-done = bf16[1,64,128,128]{3,2,0,1:T(8,128)(2,1)} async-done(((bf16[1,4,128,128]{3,2,0,1:T(8,128)(2,1)}), bf16[1,64,128,128]{3,2,0,1:T(8,128)(2,1)}) %all-gather.5.cloned.1.call-update) | async-done | bytes 2097168 | tf_op jit(solution)/shard_map/all_gather | solution.py:28
  63.1 6.2 %fusion.2 = f32[64,192,128]{2,1,0:T(8,128)} fusion(bf16[1,64,128,128]{3,2,0,1:T(8,128)(2,1)} %all-gather.5.cloned.1.call-done, bf16[64,192,128]{2,1,0:T(8,128)(2,1)} %gather_fusion.1, pred[64]{0:T(512)(128)(4,1)S(1)} %get-tuple-element.18), kind=kOutput, calls=%fused_computation.12 | convolution fusion | flops 404226048 | bytes 11534400 | tf_op jit(solution)/shard_map/tsk,skf->stf/dot_general | solution.py:38
  69.4 10.9 %scatter_fusion.1 = f32[16,192,128]{2,1,0:T(8,128)S(1)} fusion(f32[16,192,128]{2,1,0:T(8,128)S(1)} %broadcast.18.clone, s32[64]{0:T(128)S(1)} %get-tuple-element.8, f32[64,192,128]{2,1,0:T(8,128)} %fusion.2), kind=kCustom, calls=%fused_computation.5 | custom fusion | flops 1572864 | bytes 18874624 | tf_op jit(solution)/shard_map/scatter-add | solution.py:39
  80.3 34.6 %all-gather.3.cloned.1.call-done = bf16[1,64,128,128]{3,2,0,1:T(8,128)(2,1)} async-done(((bf16[1,4,128,128]{3,2,0,1:T(8,128)(2,1)}), bf16[1,64,128,128]{3,2,0,1:T(8,128)(2,1)}) %all-gather.3.cloned.1.call-update) | async-done | bytes 2097168 | tf_op jit(solution)/shard_map/all_gather | solution.py:31
  114.9 6.7 %fusion.6 = f32[64,192,128]{2,1,0:T(8,128)} fusion(bf16[1,64,128,128]{3,2,0,1:T(8,128)(2,1)} %all-gather.3.cloned.1.call-done, bf16[64,192,128]{2,1,0:T(8,128)(2,1)} %gather_fusion, pred[64]{0:T(512)(128)(4,1)S(1)} %compare_and_fusion.3), kind=kOutput, calls=%fused_computation.16 | convolution fusion | flops 404226048 | bytes 11534400 | tf_op jit(solution)/shard_map/tsk,sfk->stf/dot_general | solution.py:44
  121.7 10.6 %scatter_fusion = f32[16,192,128]{2,1,0:T(8,128)S(1)} fusion(f32[16,192,128]{2,1,0:T(8,128)S(1)} %broadcast.18.clone.1, s32[64]{0:T(128)S(1)} %get-tuple-element.6, f32[64,192,128]{2,1,0:T(8,128)} %fusion.6), kind=kCustom, calls=%fused_computation.4 | custom fusion | flops 1572864 | bytes 18874624 | tf_op jit(solution)/shard_map/scatter-add | solution.py:45
  132.4 2.3 multiply_convert_fusion
  134.7 3.7 %gather_fusion.2 = bf16[64,192,128]{2,1,0:T(8,128)(2,1)} fusion(bf16[16,192,128]{2,1,0:T(8,128)(2,1)} %get-tuple-element.12, s32[1024]{0:T(1024)S(1)} %pad_clamp_fusion.1), kind=kCustom, calls=%fused_computation.1.clone | custom fusion | bytes 6291712 | tf_op jit(solution)/shard_map/jit(_take)/gather | solution.py:47
  138.4 4.5 %convert_bitcast_fusion.1 = bf16[64,1,128,128]{3,2,0,1:T(8,128)(2,1)S(1)} fusion(bf16[64,192,128]{2,1,0:T(8,128)(2,1)} %gather_fusion.1, pred[64]{0:T(512)(128)(4,1)S(1)} %get-tuple-element.18, bf16[64,192,128]{2,1,0:T(8,128)(2,1)} %gather_fusion.2, pred[64]{0:T(512)(128)(4,1)S(1)} %get-tuple-element.17), kind=kOutput, calls=%fused_computation.30 | convolution fusion | flops 406847488 | bytes 8388736 | tf_op jit(solution)/shard_map/tsk,stf->skf/dot_general | solution.py:51
  142.9 2.6 gather_fusion.3
  145.5 4.4 %convert_bitcast_fusion = bf16[64,1,128,128]{3,2,0,1:T(8,128)(2,1)S(1)} fusion(bf16[64,192,128]{2,1,0:T(8,128)(2,1)} %gather_fusion.3, pred[64]{0:T(512)(128)(4,1)S(1)} %compare_and_fusion, bf16[64,192,128]{2,1,0:T(8,128)(2,1)} %gather_fusion, pred[64]{0:T(512)(128)(4,1)S(1)} %compare_and_fusion.3), kind=kOutput, calls=%fused_computation.29 | convolution fusion | flops 406847488 | bytes 8388736 | tf_op jit(solution)/shard_map/stf,tsk->sfk/dot_general | solution.py:52
  149.9 2.3 pad_maximum_fusion
  152.3 1.8 copy-done.3
  154.1 5.7 %fusion.10 = f32[64,192,128]{2,1,0:T(8,128)} fusion(bf16[1,64,128,128]{3,2,0,1:T(8,128)(2,1)} %all-gather.5.cloned.1.call-done, bf16[64,192,128]{2,1,0:T(8,128)(2,1)S(1)} %copy-done.3, pred[64]{0:T(512)(128)(4,1)S(1)} %get-tuple-element.17), kind=kOutput, calls=%fused_computation.25 | convolution fusion | flops 404226048 | bytes 11534400 | tf_op jit(solution)/shard_map/stf,skf->stk/dot_general | solution.py:62
  159.8 3.6 %broadcast_in_dim.23 = f32[64,192,128]{2,1,0:T(8,128)} broadcast(f32[]{:T(128)} %constant.22.clone.1), dimensions={} | broadcast | bytes 6291460 | tf_op jit(solution)/shard_map/broadcast_in_dim | solution.py:63
  163.4 16.8 %scatter_fusion.2 = f32[64,192,128]{2,1,0:T(8,128)} fusion(f32[64,192,128]{2,1,0:T(8,128)} %broadcast_in_dim.23, s32[64]{0:T(128)S(1)} %get-tuple-element.5, f32[64,192,128]{2,1,0:T(8,128)} %fusion.10), kind=kCustom, calls=%fused_computation.6 | custom fusion | flops 1572864 | bytes 18874624 | tf_op jit(solution)/shard_map/scatter-add | solution.py:63
  180.2 5.3 %convert_element_type.42 = bf16[64,192,128]{2,1,0:T(8,128)(2,1)} convert(f32[64,192,128]{2,1,0:T(8,128)} %scatter_fusion.2) | non-fusion elementwise | flops 1572864 | bytes 9437184 | tf_op jit(solution)/shard_map/convert_element_type | solution.py:65
  186.2 79.6 %all-reduce.8.cloned.1.call-done = bf16[64,2,128,128]{3,2,0,1:T(8,128)(2,1)} async-done(((bf16[64,2,128,128]{3,2,0,1:T(8,128)(2,1)}), bf16[64,2,128,128]{3,2,0,1:T(8,128)(2,1)}) %all-reduce.8.cloned.1.call-update) | async-done | bytes 4194320
  267.4 61.4 %reduce-scatter.5.cloned.1.call-done = bf16[4,192,128]{2,1,0:T(8,128)(2,1)} async-done(((bf16[64,192,128]{2,1,0:T(8,128)(2,1)}), bf16[4,192,128]{2,1,0:T(8,128)(2,1)}) %reduce-scatter.5.cloned.1.call-update) | async-done | bytes 196624 | tf_op jit(solution)/shard_map/reduce_scatter | solution.py:64
  (38 shorter events, 9.6 us)
Async XLA Ops:
  7.2 22.2 %copy-start = (bf16[192,8192]{1,0:T(8,128)(2,1)S(1)}, bf16[192,8192]{1,0:T(8,128)(2,1)}, u32[]{:S(2)}) copy-start(bf16[192,8192]{1,0:T(8,128)(2,1)} %param.12) | copy-start | bytes 9437188
  7.2 55.9 %all-gather.5.cloned.1.call-start = ((), (), s32[]{:S(2)}) async-start(), calls=%async_computation.2 | async-start | bytes 2228224 | tf_op jit(solution)/shard_map/all_gather | solution.py:28
  7.9 107.0 %all-gather.3.cloned.1.call-start = ((), (), s32[]{:S(2)}) async-start(), calls=%async_computation.1 | async-start | bytes 2228224 | tf_op jit(solution)/shard_map/all_gather | solution.py:31
  8.7 257.1 %all-reduce.8.cloned.1.call-start = ((), (), s32[]{:S(2)}) async-start(), calls=%async_computation.4 | async-start | bytes 8388608
  138.4 4.5 %copy-start.2 = (bf16[16,192,128]{2,1,0:T(8,128)(2,1)S(1)}, bf16[16,192,128]{2,1,0:T(8,128)(2,1)}, u32[]{:S(2)}) copy-start(bf16[16,192,128]{2,1,0:T(8,128)(2,1)} %get-tuple-element.11) | copy-start | bytes 2359300
  152.2 1.9 copy-start.3
  152.2 176.6 %reduce-scatter.5.cloned.1.call-start = ((), (), s32[]{:S(2)}) async-start(), calls=%async_computation.3 | async-start | bytes 3342336 | tf_op jit(solution)/shard_map/reduce_scatter | solution.py:64
  180.2 150.2 %copy-start.1 = (bf16[192,8192]{1,0:T(8,128)(2,1)S(1)}, bf16[192,8192]{1,0:T(8,128)(2,1)}, u32[]{:S(2)}) copy-start(bf16[192,8192]{1,0:T(8,128)(2,1)} %param.12) | copy-start | bytes 9437188
Sparse Core Ops, SparseCore 0:
  10.4 52.5 all-gather.4
  65.5 49.3 all-gather.2
  152.3 113.3 all-reduce.7
  268.2 60.5 reduce-scatter.4
where the time goes:
time: 338 us; the launch traced here: 337 us
  waiting for transfers between devices  198 us (59%)
  other arithmetic  48.2 us (14%)
  local copies, waits for them, and re-layouts  32.1 us (9%)
  matrix products  27.5 us (8%)
  blocking collectives  15.6 us (5%)
  between operations  15.2 us (4%)
    unnamed x5, waiting for transfers between devices  81 us
    reduce_scatter x1, waiting for transfers between devices, on_device(): lax.psum_scatter(in_part.astype(jnp.bfloat16), 'tensor', scatter_dimensio...  61.4 us
    all_gather x1, waiting for transfers between devices, on_device(): lax.all_gather(down_tiles, 'fsdp', axis=1, tiled=True)  34.6 us
    all_gather x1, waiting for transfers between devices, on_device(): lax.all_gather(up_tiles, 'fsdp', axis=1, tiled=True)  21.2 us
    scatter-add x1, other arithmetic, on_device(): in_part = jax.ops.segment_sum(back_in, r_up, num_segments=row_blocks)  16.8 us
    another operation x1, blocking collectives, on_device(): in_part = jax.ops.segment_sum(back_in, r_up, num_segments=row_blocks)  15.6 us
    scatter-add x1, other arithmetic, on_device(): pre = jax.ops.segment_sum(prod, c_up, num_segments=group_cols)  10.9 us
    scatter-add x1, other arithmetic, on_device(): dhid = jax.ops.segment_sum(back, r_down, num_segments=group_cols)  10.6 us
  transfers between devices with their start and end apart: 4, of which 4 were waited for; matrix products, arithmetic and copies ran while one was open for 20% of the time, Pallas kernels for 0%

commit v1 on v0

--- a/solution.py
+++ b/solution.py
@@ -5,6 +5,18 @@
 
 FF = 32768
 TILE = 128
+
+
+def _mix_sample(x0, shard_axis):
+    return jnp.concatenate(
+        lax.all_to_all(
+            jnp.stack([x0] * lax.axis_size(shard_axis), axis=0),
+            axis_name=shard_axis,
+            split_axis=0,
+            concat_axis=0,
+        ),
+        axis=1,
+    )
 
 
 def gelu_parts(pre):
@@ -25,7 +37,7 @@
     input_blocks = inputs.reshape(tok_count, row_blocks, TILE)
     cotan_blocks = cotangent.reshape(tok_count, row_blocks, TILE)
     gathered = (
-        lax.all_gather(up_tiles, "fsdp", axis=1, tiled=True),
+        _mix_sample(up_tiles, "fsdp"),
         lax.all_gather(up_rows, "fsdp", axis=1, tiled=True),
         lax.all_gather(up_cols, "fsdp", axis=1, tiled=True),
         lax.all_gather(down_tiles, "fsdp", axis=1, tiled=True),

time: 338 us -> 310 us (0.917)
  waiting for transfers between devices: 198 us -> 143 us
  blocking collectives: 15.6 us -> 36.4 us
  starting transfers between devices: 0.16 us -> 7.59 us
    all_gather x1, waiting for transfers between devices: 34.6 us -> 0.02 us  [on_device(): lax.all_gather(down_tiles, 'fsdp', axis=1, tiled=True)]
    all_gather x1 -> x0, waiting for transfers between devices: 21.2 us -> none  [on_device(): lax.all_gather(up_tiles, 'fsdp', axis=1, tiled=True)]
    another operation x1, blocking collectives: 15.6 us -> 36.4 us  [on_device(): in_part = jax.ops.segment_sum(back_in, r_up, num_segments=row_blocks)]
    all_to_all x0 -> x1, starting transfers between devices: none -> 7.48 us  [_mix_sample(): lax.all_to_all(jnp.stack([x0] * lax.axis_size(shard_axis), axis=0), axis_...]
    unnamed x5 -> x4, waiting for transfers between devices: 81 us -> 81.1 us
  transfers between devices with their start and end apart: 4 -> 4, of which waited for: 4 -> 2; matrix products, arithmetic and copies ran while one was open for 20% -> 21% of each run, Pallas kernels for 0% -> 0%
where the time goes in v1:
time: 310 us; the launch traced here: 309 us
  waiting for transfers between devices  143 us (46%)
  other arithmetic  48.1 us (16%)
  blocking collectives  36.4 us (12%)
  local copies, waits for them, and re-layouts  31.5 us (10%)
  matrix products  27.7 us (9%)
  between operations  15.3 us (5%)
  starting transfers between devices  7.59 us (2%)
    unnamed x4, waiting for transfers between devices  81.1 us
    reduce_scatter x1, waiting for transfers between devices, on_device(): lax.psum_scatter(in_part.astype(jnp.bfloat16), 'tensor', scatter_dimensio...  61.5 us
    another operation x1, blocking collectives, on_device(): in_part = jax.ops.segment_sum(back_in, r_up, num_segments=row_blocks)  36.4 us
    scatter-add x1, other arithmetic, on_device(): in_part = jax.ops.segment_sum(back_in, r_up, num_segments=row_blocks)  16.8 us
    scatter-add x1, other arithmetic, on_device(): pre = jax.ops.segment_sum(prod, c_up, num_segments=group_cols)  10.8 us
    scatter-add x1, other arithmetic, on_device(): dhid = jax.ops.segment_sum(back, r_down, num_segments=group_cols)  10.6 us
    all_to_all x1, starting transfers between devices, _mix_sample(): lax.all_to_all(jnp.stack([x0] * lax.axis_size(shard_axis), axis=0), axis_...  7.48 us
    dot_general x1, matrix products, on_device(): jnp.einsum('tsk,sfk->stf', dy_sel, w_down, preferred_element_type=jnp.flo...  6.72 us
  transfers between devices with their start and end apart: 4, of which 2 were waited for; matrix products, arithmetic and copies ran while one was open for 21% of the time, Pallas kernels for 0%

profile of v1, /device:TPU:2, one launch (start us, length us, event | category | flops | bytes accessed | tf_op | source)
XLA Modules:
  0.0 309.2 jit_solution(11609422963560149094)
XLA Ops:
  7.2 2.9 stack.11
  10.2 7.5 %all-to-all-start = ((bf16[16,1,4,128,128]{4,3,2,1,0:T(8,128)(2,1)}), bf16[16,1,4,128,128]{4,3,2,1,0:T(8,128)(2,1)}, u32[]{:S(2)}, u32[]{:S(2)}) async-start(bf16[16,1,4,128,128]{4,3,2,1,0:T(8,128)(2,1)} %stack.11), calls=%async_computation | async-start | bytes 4194304 | tf_op jit(solution)/shard_map/all_to_all | solution.py:12
  20.1 36.4 %all-reduce.5 = (s32[64]{0:T(128)S(1)}, s32[64]{0:T(128)S(1)}, s32[64]{0:T(128)S(1)}, s32[64]{0:T(128)S(1)}) all-reduce(s32[64]{0:T(128)S(1)} %bitcast_dynamic-update-slice_fusion.3, s32[64]{0:T(128)S(1)} %bitcast_dynamic-update-slice_fusion.1, s32[64]{0:T(128)S(1)} %bitcast_dynamic-update-slice_fusion, ...), channel_id=1, replica_groups=mesh['fsdp'=16,'tensor'=16] {'fsdp'}, use_global_device_ids=true, to_apply=%add | all-reduce | flops 256 | bytes 2048 | tf_op jit(solution)/shard_map/broadcast_in_dim;squeeze | solution.py:75
  56.5 2.5 copy_bitcast_fusion
  59.0 4.5 %gather_fusion.1 = bf16[64,192,128]{2,1,0:T(8,128)(2,1)} fusion(bf16[192,64,128]{2,0,1:T(8,128)(2,1)} %copy_bitcast_fusion, s32[1024]{0:T(1024)S(1)} %pad_clamp_fusion.2), kind=kCustom, calls=%fused_computation.2.clone | custom fusion | bytes 6291712 | tf_op jit(solution)/shard_map/jit(_take)/gather | solution.py:49
  63.5 2.8 copy_bitcast_fusion.1
  66.3 2.7 gather_fusion
  69.1 6.3 %fusion.2 = f32[64,192,128]{2,1,0:T(8,128)} fusion(bf16[64,128,128]{2,1,0:T(8,128)(2,1)} %bitcast.10, bf16[64,192,128]{2,1,0:T(8,128)(2,1)} %gather_fusion.1, pred[64]{0:T(512)(128)(4,1)S(1)} %get-tuple-element.18), kind=kOutput, calls=%fused_computation.12 | convolution fusion | flops 404226048 | bytes 11534400 | tf_op jit(solution)/shard_map/tsk,skf->stf/dot_general | solution.py:50
  75.6 10.8 %scatter_fusion.1 = f32[16,192,128]{2,1,0:T(8,128)S(1)} fusion(f32[16,192,128]{2,1,0:T(8,128)S(1)} %broadcast.21.clone, s32[64]{0:T(128)S(1)} %get-tuple-element.8, f32[64,192,128]{2,1,0:T(8,128)} %fusion.2), kind=kCustom, calls=%fused_computation.5 | custom fusion | flops 1572864 | bytes 18874624 | tf_op jit(solution)/shard_map/scatter-add | solution.py:51
  86.4 6.7 %fusion.6 = f32[64,192,128]{2,1,0:T(8,128)} fusion(bf16[1,64,128,128]{3,2,0,1:T(8,128)(2,1)} %all-gather.2.cloned.1.call-done, bf16[64,192,128]{2,1,0:T(8,128)(2,1)} %gather_fusion, pred[64]{0:T(512)(128)(4,1)S(1)} %compare_and_fusion.3), kind=kOutput, calls=%fused_computation.16 | convolution fusion | flops 404226048 | bytes 11534400 | tf_op jit(solution)/shard_map/tsk,sfk->stf/dot_general | solution.py:56
  93.3 10.6 %scatter_fusion = f32[16,192,128]{2,1,0:T(8,128)S(1)} fusion(f32[16,192,128]{2,1,0:T(8,128)S(1)} %broadcast.21.clone.1, s32[64]{0:T(128)S(1)} %get-tuple-element.6, f32[64,192,128]{2,1,0:T(8,128)} %fusion.6), kind=kCustom, calls=%fused_computation.4 | custom fusion | flops 1572864 | bytes 18874624 | tf_op jit(solution)/shard_map/scatter-add | solution.py:57
  103.9 2.3 multiply_convert_fusion
  106.2 3.7 %gather_fusion.2 = bf16[64,192,128]{2,1,0:T(8,128)(2,1)} fusion(bf16[16,192,128]{2,1,0:T(8,128)(2,1)} %get-tuple-element.12, s32[1024]{0:T(1024)S(1)} %pad_clamp_fusion.1), kind=kCustom, calls=%fused_computation.1.clone | custom fusion | bytes 6291712 | tf_op jit(solution)/shard_map/jit(_take)/gather | solution.py:59
  109.9 4.5 %convert_bitcast_fusion.1 = bf16[64,1,128,128]{3,2,0,1:T(8,128)(2,1)S(1)} fusion(bf16[64,192,128]{2,1,0:T(8,128)(2,1)} %gather_fusion.1, pred[64]{0:T(512)(128)(4,1)S(1)} %get-tuple-element.18, bf16[64,192,128]{2,1,0:T(8,128)(2,1)} %gather_fusion.2, pred[64]{0:T(512)(128)(4,1)S(1)} %get-tuple-element.17), kind=kOutput, calls=%fused_computation.27 | convolution fusion | flops 406847488 | bytes 8388736 | tf_op jit(solution)/shard_map/tsk,stf->skf/dot_general | solution.py:63
  114.4 2.6 gather_fusion.3
  117.1 4.4 %convert_bitcast_fusion = bf16[64,1,128,128]{3,2,0,1:T(8,128)(2,1)S(1)} fusion(bf16[64,192,128]{2,1,0:T(8,128)(2,1)} %gather_fusion.3, pred[64]{0:T(512)(128)(4,1)S(1)} %compare_and_fusion, bf16[64,192,128]{2,1,0:T(8,128)(2,1)} %gather_fusion, pred[64]{0:T(512)(128)(4,1)S(1)} %compare_and_fusion.3), kind=kOutput, calls=%fused_computation.26 | convolution fusion | flops 406847488 | bytes 8388736 | tf_op jit(solution)/shard_map/stf,tsk->sfk/dot_general | solution.py:64
  121.5 2.3 pad_maximum_fusion
  123.8 1.8 copy-done.3
  125.7 5.8 %fusion.25 = f32[64,192,128]{2,1,0:T(8,128)} fusion(bf16[64,128,128]{2,1,0:T(8,128)(2,1)} %bitcast.10, bf16[64,192,128]{2,1,0:T(8,128)(2,1)S(1)} %copy-done.3, pred[64]{0:T(512)(128)(4,1)S(1)} %get-tuple-element.17), kind=kOutput, calls=%fused_computation.37 | convolution fusion | flops 404226048 | bytes 11534400 | tf_op jit(solution)/shard_map/stf,skf->stk/dot_general | solution.py:74
  131.4 3.4 %broadcast_in_dim.23 = f32[64,192,128]{2,1,0:T(8,128)} broadcast(f32[]{:T(128)} %constant.22.clone.1), dimensions={} | broadcast | bytes 6291460 | tf_op jit(solution)/shard_map/broadcast_in_dim | solution.py:75
  134.8 16.8 %scatter_fusion.2 = f32[64,192,128]{2,1,0:T(8,128)} fusion(f32[64,192,128]{2,1,0:T(8,128)} %broadcast_in_dim.23, s32[64]{0:T(128)S(1)} %get-tuple-element.5, f32[64,192,128]{2,1,0:T(8,128)} %fusion.25), kind=kCustom, calls=%fused_computation.6 | custom fusion | flops 1572864 | bytes 18874624 | tf_op jit(solution)/shard_map/scatter-add | solution.py:75
  151.6 5.3 %convert_element_type.42 = bf16[64,192,128]{2,1,0:T(8,128)(2,1)} convert(f32[64,192,128]{2,1,0:T(8,128)} %scatter_fusion.2) | non-fusion elementwise | flops 1572864 | bytes 9437184 | tf_op jit(solution)/shard_map/convert_element_type | solution.py:77
  157.5 80.4 %all-reduce.8.cloned.1.call-done = bf16[64,2,128,128]{3,2,0,1:T(8,128)(2,1)} async-done(((bf16[64,2,128,128]{3,2,0,1:T(8,128)(2,1)}), bf16[64,2,128,128]{3,2,0,1:T(8,128)(2,1)}) %all-reduce.8.cloned.1.call-update) | async-done | bytes 4194320
  239.6 61.5 %reduce-scatter.5.cloned.1.call-done = bf16[4,192,128]{2,1,0:T(8,128)(2,1)} async-done(((bf16[64,192,128]{2,1,0:T(8,128)(2,1)}), bf16[4,192,128]{2,1,0:T(8,128)(2,1)}) %reduce-scatter.5.cloned.1.call-update) | async-done | bytes 196624 | tf_op jit(solution)/shard_map/reduce_scatter | solution.py:76
  (48 shorter events, 5.5 us)
Async XLA Ops:
  7.2 49.3 %copy-start = (bf16[192,8192]{1,0:T(8,128)(2,1)S(1)}, bf16[192,8192]{1,0:T(8,128)(2,1)}, u32[]{:S(2)}) copy-start(bf16[192,8192]{1,0:T(8,128)(2,1)} %param.12) | copy-start | bytes 9437188
  7.2 11.2 %copy-start.4 = (u32[256]{0:T(256)S(1)}, u32[256]{0:T(256)}, u32[]{:S(2)}) copy-start(u32[256]{0:T(256)} %constant.41) | copy-start | bytes 3076
  7.2 12.5 %copy-start.5 = (s32[1,4]{1,0:T(1,128)S(1)}, s32[1,4]{1,0:T(1,128)}, u32[]{:S(2)}) copy-start(s32[1,4]{1,0:T(1,128)} %param.19) | copy-start | bytes 52
  7.2 12.6 %copy-start.6 = (s32[1,4]{1,0:T(1,128)S(1)}, s32[1,4]{1,0:T(1,128)}, u32[]{:S(2)}) copy-start(s32[1,4]{1,0:T(1,128)} %param.18) | copy-start | bytes 52
  7.2 12.7 %copy-start.7 = (s32[1,4]{1,0:T(1,128)S(1)}, s32[1,4]{1,0:T(1,128)}, u32[]{:S(2)}) copy-start(s32[1,4]{1,0:T(1,128)} %param.16) | copy-start | bytes 52
  7.2 12.8 %copy-start.8 = (s32[1,4]{1,0:T(1,128)S(1)}, s32[1,4]{1,0:T(1,128)}, u32[]{:S(2)}) copy-start(s32[1,4]{1,0:T(1,128)} %param.15) | copy-start | bytes 52
  10.2 58.9 %all-to-all-start = ((bf16[16,1,4,128,128]{4,3,2,1,0:T(8,128)(2,1)}), bf16[16,1,4,128,128]{4,3,2,1,0:T(8,128)(2,1)}, u32[]{:S(2)}, u32[]{:S(2)}) async-start(bf16[16,1,4,128,128]{4,3,2,1,0:T(8,128)(2,1)} %stack.11), calls=%async_computation | async-start | bytes 4194304 | tf_op jit(solution)/shard_map/all_to_all | solution.py:12
  17.6 68.8 %all-gather.2.cloned.1.call-start = ((), (), s32[]{:S(2)}) async-start(), calls=%async_computation.2 | async-start | bytes 2228224 | tf_op jit(solution)/shard_map/all_gather | solution.py:43
  18.4 219.5 %all-reduce.8.cloned.1.call-start = ((), (), s32[]{:S(2)}) async-start(), calls=%async_computation.4 | async-start | bytes 8388608
  109.9 4.5 %copy-start.2 = (bf16[16,192,128]{2,1,0:T(8,128)(2,1)S(1)}, bf16[16,192,128]{2,1,0:T(8,128)(2,1)}, u32[]{:S(2)}) copy-start(bf16[16,192,128]{2,1,0:T(8,128)(2,1)} %get-tuple-element.11) | copy-start | bytes 2359300
  123.8 1.9 copy-start.3
  123.8 177.3 %reduce-scatter.5.cloned.1.call-start = ((), (), s32[]{:S(2)}) async-start(), calls=%async_computation.3 | async-start | bytes 3342336 | tf_op jit(solution)/shard_map/reduce_scatter | solution.py:76
  151.6 151.1 %copy-start.1 = (bf16[192,8192]{1,0:T(8,128)(2,1)S(1)}, bf16[192,8192]{1,0:T(8,128)(2,1)}, u32[]{:S(2)}) copy-start(bf16[192,8192]{1,0:T(8,128)(2,1)} %param.12) | copy-start | bytes 9437188
Sparse Core Ops, SparseCore 0:
  20.9 58.6 all-gather.1
  123.9 113.9 all-reduce.7
  240.4 60.5 reduce-scatter.4
